TPU v7x, 128 devices: a whole 4x4x4 slice. The times are simulated.
128 devices in a mesh: sec: 4 (over y), dp: 8 (over x_hi, z), mp: 4 (over x_lo, core).
Axes of the slice: x: 4 (x_hi: 2, x_lo: 2; x = x_hi * 2 + x_lo), y: 4, z: 4, core: 2. Of those that a mesh axis runs over, the one named last changes fastest.
Arguments:
- patches: bfloat16 [320, 5120], P('dp'), may hold values from -6 to 6
- ln_gain: bfloat16 [1280], replicated, may hold values from 0.099609375 to 1.8984375
- ln_shift: bfloat16 [1280], replicated, may hold values from -3 to 3
- w_in: bfloat16 [5120, 5120], P('dp', ('sec', 'mp')), may hold values from -0.078125 to 0.078125
- b_in: bfloat16 [5120], P(('sec', 'mp')), may hold values from -3 to 3
- w_out: bfloat16 [5120, 8192], P(('sec', 'mp'), 'dp'), may hold values from -0.125 to 0.125
- b_out: bfloat16 [8192], P(('sec', 'mp')), may hold values from -3 to 3
- place: int32 [320], P('dp'), may hold values from 0 to 255, as said below
- image_counts: int32 [8], P('dp'), may hold values from 1 to 40, 128 in all
- text_rows: bfloat16 [2048, 8192], P('dp', ('sec', 'mp')), may hold values from -6 to 6
- segments: int32 [8, 256], P('dp'), may hold values from 0 to 3, never falling along the last dimension, each value on 1 to 128 neighbouring positions
- norm_gain: bfloat16 [2, 8192], replicated, may hold values from 0.099609375 to 1.8984375
- q_weight: bfloat16 [2, 8192, 4096], P(None, None, ('sec', 'mp'))
- kv_weight: bfloat16 [2, 2, 512, 8192], P(None, None, ('sec', 'mp'))
- o_weight: bfloat16 [2, 4096, 8192], P(None, ('sec', 'mp')), may hold values from -0.125 to 0.125
- grad_rows: bfloat16 [320, 8192], P('dp'), may hold values from -6 to 6
Outputs:
- final_rows: float32 [2048, 8192], P('dp', ('sec', 'mp'))
- patch_grads: float32 [320, 5120], P('dp')
Inputs may be any that keep to these rules, and one draw needn't show every extreme that they name: `place`: each owner's 40 entries are distinct token positions of its own packed sequence; only an owner's first image_counts entries are used. `image_counts`: the counts sum to 8 * (16) over all owners.
All inputs are finite; a program needn't handle non-finite values. No bound on the sum of `image_counts` on one device may be relied on, other than what follows from the above.
Results may differ from a plain program's by a relative error of at most 0.0055.
Values may be sent and summed in bfloat16 or wider, within the bound.
A program may use at most 128 MiB of HBM per device.

v0:
```python
import math
import jax
import jax.numpy as jnp
from jax import lax
from jax.sharding import PartitionSpec as P

D = 8192
HEAD_DIM = 128
ln_eps = 1e-06
rms_eps = 1e-06
rope_base = 1000000.0


def group_norm(patch_rows, ln_gain, ln_shift):
    row_count = patch_rows.shape[0]
    grouped = patch_rows.astype(jnp.float32).reshape(row_count, -1, ln_gain.shape[0])
    center = grouped - jnp.mean(grouped, axis=-1, keepdims=True)
    spread = jnp.mean(center * center, axis=-1, keepdims=True)
    scaled = center * lax.rsqrt(spread + ln_eps) * ln_gain.astype(jnp.float32) + ln_shift.astype(
        jnp.float32
    )
    return scaled.reshape(row_count, -1)


def gelu_exact(values):
    return jax.nn.gelu(values, approximate=False)


def rotate(values, positions):
    head_depth = values.shape[-1]
    half_depth = head_depth // 2
    inv_freq = rope_base ** (-2.0 * jnp.arange(half_depth, dtype=jnp.float32) / head_depth)
    angles = positions[:, None] * inv_freq[None, :]
    cosine = jnp.cos(angles)[:, None, :]
    sine_part = jnp.sin(angles)[:, None, :]
    first_half = values[..., :half_depth]
    second = values[..., half_depth:]
    return jnp.concatenate(
        [first_half * cosine - second * sine_part, second * cosine + first_half * sine_part],
        axis=-1,
    )


def doc_mask(segment_ids):
    token_index = jnp.arange(segment_ids.shape[0], dtype=jnp.int32)
    same_doc = segment_ids[:, None] == segment_ids[None, :]
    allowed = same_doc & (token_index[None, :] <= token_index[:, None])
    positions = jnp.sum(allowed.astype(jnp.int32), axis=1) - 1
    return (allowed, positions.astype(jnp.float32))


def attend(normed, allowed, positions, q_local, kv_local):
    token_count = normed.shape[0]
    queries = jnp.dot(normed, q_local, preferred_element_type=jnp.float32).reshape(
        token_count, -1, HEAD_DIM
    )
    key_value = jnp.einsum("td,kcd->tkc", normed, kv_local, preferred_element_type=jnp.float32)
    key_value = lax.all_gather(key_value, "mp", axis=2, tiled=True)
    key_rows = rotate(key_value[:, 0:1, :], positions)[:, 0, :].astype(jnp.bfloat16)
    value_rows = key_value[:, 1, :].astype(jnp.bfloat16)
    queries = rotate(queries, positions).astype(jnp.bfloat16)
    scores = jnp.einsum("thd,sd->hts", queries, key_rows, preferred_element_type=jnp.float32) * (
        1.0 / math.sqrt(HEAD_DIM)
    )
    scores = jnp.where(allowed[None], scores, -jnp.inf)
    row_max = jnp.max(scores, axis=-1, keepdims=True)
    exp_scores = jnp.exp(scores - row_max)
    attn_weights = (exp_scores / jnp.sum(exp_scores, axis=-1, keepdims=True)).astype(jnp.bfloat16)
    attended = jnp.einsum(
        "hts,sd->thd", attn_weights, value_rows, preferred_element_type=jnp.float32
    )
    return attended.astype(jnp.bfloat16).reshape(token_count, -1)


def gather_features(rows_local):
    return lax.all_gather(rows_local, ("sec", "mp"), axis=1, tiled=True)


def section_features(rows_local, gain_row, allowed, positions, q_local, kv_local, o_local):
    share = rows_local.shape[1]
    square_sums = lax.psum(jnp.sum(rows_local * rows_local, axis=1), ("sec", "mp"))
    factor = lax.rsqrt(square_sums / D + rms_eps)
    gain_local = lax.dynamic_slice_in_dim(
        gain_row, lax.axis_index(("sec", "mp")) * share, share, 0
    ).astype(jnp.float32)
    normed_local = (rows_local * factor[:, None] * gain_local[None, :]).astype(jnp.bfloat16)
    normed = gather_features(normed_local)
    attended = attend(normed, allowed, positions, q_local, kv_local)
    summed = lax.psum_scatter(
        lax.dot_general(
            o_local, attended, (((0,), (1,)), ((), ())), preferred_element_type=jnp.float32
        ),
        ("sec", "mp"),
        scatter_dimension=0,
        tiled=True,
    )
    return rows_local + summed.T


def merger_front(patch_rows, ln_gain, ln_shift, w_in_full, b_in, w_out_full, b_out):
    normed = group_norm(patch_rows, ln_gain, ln_shift).astype(jnp.bfloat16)
    pre_act = jnp.dot(normed, w_in_full, preferred_element_type=jnp.float32) + b_in.astype(
        jnp.float32
    )
    hidden_units = gelu_exact(pre_act).astype(jnp.bfloat16)
    partial_out = jnp.dot(hidden_units, w_out_full, preferred_element_type=jnp.float32)
    merged = lax.psum_scatter(
        partial_out, ("sec", "mp"), scatter_dimension=1, tiled=True
    ) + b_out.astype(jnp.float32)
    return (merged.astype(jnp.bfloat16), pre_act)


def merger_back(patch_rows, pre_act, hidden_grads, ln_gain, ln_shift, w_in_full):
    _, pull_gelu = jax.vjp(gelu_exact, pre_act)
    pre_grads = pull_gelu(hidden_grads)[0].astype(jnp.bfloat16)
    normed_grads = lax.dot_general(
        pre_grads, w_in_full, (((1,), (1,)), ((), ())), preferred_element_type=jnp.float32
    )
    normed_grads = lax.psum(normed_grads, ("sec", "mp"))
    _, pull_norm = jax.vjp(
        lambda values: group_norm(values, ln_gain, ln_shift), patch_rows.astype(jnp.float32)
    )
    return pull_norm(normed_grads)[0]


def local(
    patches,
    ln_gain,
    ln_shift,
    w_in,
    b_in,
    w_out,
    b_out,
    place,
    image_counts,
    text_rows,
    segments,
    norm_gain,
    q_weight,
    kv_weight,
    o_weight,
    grad_rows,
):
    w_in_full, w_out_full = (
        lax.all_gather(w_in, "dp", axis=0, tiled=True),
        lax.all_gather(w_out, "dp", axis=1, tiled=True),
    )
    slot_count = patches.shape[0]
    tokens = text_rows.shape[0]
    slot_index = jnp.arange(slot_count, dtype=jnp.int32)
    live_slot = slot_index < image_counts[0]
    slot_grads = jnp.where(live_slot[:, None], grad_rows, jnp.zeros_like(grad_rows))
    hidden_grads = lax.dot_general(
        slot_grads, w_out_full, (((1,), (1,)), ((), ())), preferred_element_type=jnp.float32
    )
    merged_local, pre_act = merger_front(
        patches, ln_gain, ln_shift, w_in_full, b_in, w_out_full, b_out
    )
    patch_grads = merger_back(patches, pre_act, hidden_grads, ln_gain, ln_shift, w_in_full)
    token_index = jnp.arange(tokens, dtype=jnp.int32)
    select = (place[:, None] == token_index[None, :]) & live_slot[:, None]
    is_image = jnp.any(select, axis=0)
    picked = lax.dot_general(
        select.astype(jnp.bfloat16),
        merged_local,
        (((0,), (0,)), ((), ())),
        preferred_element_type=jnp.float32,
    )
    start_rows = jnp.where(is_image[:, None], picked, text_rows.astype(jnp.float32)).astype(
        jnp.bfloat16
    )
    allowed, positions = doc_mask(segments[0])
    layer_count = q_weight.shape[0]
    current = start_rows.astype(jnp.float32)
    for layer_index in range(layer_count):
        current = section_features(
            current,
            norm_gain[layer_index],
            allowed,
            positions,
            q_weight[layer_index],
            kv_weight[layer_index],
            o_weight[layer_index],
        )
    return (current, patch_grads)


def solution(mesh):
    in_specs = (
        P("dp", None),
        P(),
        P(),
        P("dp", ("sec", "mp")),
        P(("sec", "mp")),
        P(("sec", "mp"), "dp"),
        P(("sec", "mp")),
        P("dp"),
        P("dp"),
        P("dp", ("sec", "mp")),
        P("dp", None),
        P(),
        P(None, None, ("sec", "mp")),
        P(None, None, ("sec", "mp"), None),
        P(None, ("sec", "mp"), None),
        P("dp", None),
    )
    out_specs = (P("dp", ("sec", "mp")), P("dp", None))
    return jax.shard_map(local, mesh=mesh, in_specs=in_specs, out_specs=out_specs, check_vma=False)
```

profile of v0, /device:TPU:0, one launch (start us, length us, event | category | flops | bytes accessed | tf_op | source)
XLA Modules:
  0.0 707.5 jit_solution(7781813747117255810)
XLA Ops:
  7.2 0.7 all-gather.5.cloned.1.call-update
  8.0 0.7 all-gather.7.cloned.1.call-update
  8.7 1.4 reshape.223
  10.2 0.2 reduce_sum.78
  10.4 0.4 multiply_reduce_fusion.1
  10.7 0.2 mul.308
  10.9 0.1 copy.43
  11.1 0.2 sub.50
  11.3 0.1 copy.42
  11.5 64.8 %all-gather.5.cloned.1.call-done = bf16[5120,320]{0,1:T(8,128)(2,1)} async-done(((bf16[640,320]{0,1:T(8,128)(2,1)}), bf16[5120,320]{0,1:T(8,128)(2,1)}) %all-gather.5.cloned.1.call-update) | async-done | bytes 3276816 | tf_op jit(solution)/shard_map/all_gather | solution.py:145
  76.3 3.0 convolution_add_fusion
  79.4 77.0 %all-gather.7.cloned.1.call-done = bf16[320,8192]{1,0:T(8,128)(2,1)} async-done(((bf16[320,1024]{1,0:T(8,128)(2,1)}), bf16[320,8192]{1,0:T(8,128)(2,1)}) %all-gather.7.cloned.1.call-update) | async-done | bytes 5242896 | tf_op jit(solution)/shard_map/all_gather | solution.py:146
  156.4 4.6 fusion.88
  161.1 0.0 all-gather.9.cloned.1.call-start
  161.9 0.1 fusion.116
  161.9 0.1 fusion.87
  162.0 60.0 %reduce-scatter.4.cloned.1.call-done = f32[40,512]{1,0:T(8,128)} async-done(((f32[40,8192]{1,0:T(8,128)}), f32[40,512]{1,0:T(8,128)}) %reduce-scatter.4.cloned.1.call-update) | async-done | bytes 81936 | tf_op jit(solution)/shard_map/reduce_scatter | solution.py:107
  222.0 1.4 multiply_reduce_fusion.3
  223.4 27.7 %psum.21 = f32[256]{0:T(256)S(1)} all-reduce(f32[256]{0:T(256)S(1)} %get-tuple-element.16), channel_id=1, replica_groups=mesh['sec'=4,'dp'=8,'mp'=4] {'sec','mp'}, use_global_device_ids=true, to_apply=%region_5.6 | all-reduce | flops 256 | bytes 2048 | tf_op jit(solution)/shard_map/psum | solution.py:81
  251.1 0.8 multiply_convert_fusion.1
  252.0 0.0 reduce-scatter.6.cloned.1.call-start
  252.0 5.7 slice_bitcast_fusion.1
  257.8 6.4 copy.26
  264.2 0.1 convert_reduce_fusion
  264.3 0.1 fusion.36
  264.5 0.3 multiply_cosine_fusion
  264.8 23.3 %all-gather.9.cloned.1.call-done = bf16[256,8192]{1,0:T(8,128)(2,1)} async-done(((bf16[256,512]{1,0:T(8,128)(2,1)}), bf16[256,8192]{1,0:T(8,128)(2,1)}) %all-gather.9.cloned.1.call-update) | async-done | bytes 4194320 | tf_op jit(solution)/shard_map/all_gather | solution.py:76
  288.1 4.0 fusion.10
  292.1 5.8 all_gather.21
  297.9 0.3 fusion.52
  298.3 3.5 fusion.8
  301.8 0.6 copy-done.12
  302.4 1.0 fusion.21
  303.5 1.2 fusion.117
  304.7 1.6 convolution_convert_fusion.1
  306.3 6.7 convolution_bitcast_fusion.1
  313.1 97.8 %reduce-scatter.6.cloned.1.call-done = f32[512,256]{0,1:T(8,128)} async-done(((f32[8192,256]{0,1:T(8,128)}), f32[512,256]{0,1:T(8,128)}) %reduce-scatter.6.cloned.1.call-update) | async-done | bytes 524304 | tf_op jit(solution)/shard_map/reduce_scatter | solution.py:89
  410.9 1.2 multiply_reduce_fusion.2
  412.1 27.6 %psum.22 = f32[256]{0:T(256)S(1)} all-reduce(f32[256]{0:T(256)S(1)} %multiply_reduce_fusion.2), channel_id=1, replica_groups=mesh['sec'=4,'dp'=8,'mp'=4] {'sec','mp'}, use_global_device_ids=true, to_apply=%region_11.12 | all-reduce | flops 256 | bytes 2048 | tf_op jit(solution)/shard_map/psum | solution.py:81
  439.7 1.9 multiply_convert_fusion
  441.6 0.2 all-reduce.2.cloned.1.call-start
  441.8 6.5 copy.30
  448.3 7.6 %fusion.71 = f32[40,5120]{1,0:T(8,128)} fusion(bf16[5120,320]{0,1:T(8,128)(2,1)} %all-gather.5.cloned.1.call-done, bf16[320,8192]{1,0:T(8,128)(2,1)} %all-gather.7.cloned.1.call-done, bf16[40,8192]{1,0:T(8,128)(2,1)S(1)} %copy-done.7, pred[40]{0:T(512)(128)(4,1)S(1)} %iota_compare_fusion.2, f32[40,320]{1,0:T(8,128)S(1)} %convolution_add_fusion), kind=kOutput, calls=%fused_computation.107 | convolution fusion | flops 342036480 | bytes 10045480 | tf_op jit(solution)/shard_map/dot_general | solution.py:116
  456.0 21.5 %all-gather.11.cloned.1.call-done = bf16[256,8192]{1,0:T(8,128)(2,1)} async-done(((bf16[256,512]{1,0:T(8,128)(2,1)}), bf16[256,8192]{1,0:T(8,128)(2,1)}) %all-gather.11.cloned.1.call-update) | async-done | bytes 4194320 | tf_op jit(solution)/shard_map/all_gather | solution.py:76
  477.5 4.0 fusion.5
  481.5 5.8 all_gather.23
  487.3 0.3 fusion.56
  487.6 3.5 fusion.3
  491.2 0.6 copy-done.11
  491.8 1.0 fusion.19
  492.9 1.2 fusion.120
  494.1 1.6 convolution_convert_fusion
  495.7 6.7 convolution_bitcast_fusion
  502.4 97.3 %all-reduce.2.cloned.1.call-done = f32[40,5120]{1,0:T(8,128)} async-done(((f32[40,5120]{1,0:T(8,128)}), f32[40,5120]{1,0:T(8,128)}) %all-reduce.2.cloned.1.call-update) | async-done | bytes 819216 | tf_op jit(solution)/shard_map/psum | solution.py:119
  599.7 1.5 reshape.226
  601.3 0.4 multiply_reduce_fusion
  601.7 0.6 fusion.29
  602.3 0.2 broadcast_in_dim.45
  602.5 0.1 copy.45
  602.6 0.2 broadcast_in_dim.43
  602.8 0.1 copy.44
  603.0 1.2 fusion.28
  604.2 94.5 %reduce-scatter.8.cloned.1.call-done = f32[512,256]{0,1:T(8,128)} async-done(((f32[8192,256]{0,1:T(8,128)}), f32[512,256]{0,1:T(8,128)}) %reduce-scatter.8.cloned.1.call-update) | async-done | bytes 524304 | tf_op jit(solution)/shard_map/reduce_scatter | solution.py:89
  698.7 2.0 bitcast_add_fusion
  (71 shorter events, 0.6 us)
Async XLA Ops:
  7.2 69.2 %all-gather.5.cloned.1.call-start = ((), (), s32[]{:S(2)}) async-start(), calls=%async_computation.3 | async-start | bytes 3686400 | tf_op jit(solution)/shard_map/all_gather | solution.py:145
  7.9 3.5 copy-start.16
  7.9 3.6 copy-start.17
  7.9 148.5 %all-gather.7.cloned.1.call-start = ((), (), s32[]{:S(2)}) async-start(), calls=%async_computation.4 | async-start | bytes 5898240 | tf_op jit(solution)/shard_map/all_gather | solution.py:146
  8.7 2.8 copy-start.18
  8.7 67.7 %copy-start.5 = (bf16[40,5120]{1,0:T(8,128)(2,1)S(1)}, bf16[40,5120]{1,0:T(8,128)(2,1)}, u32[]{:S(2)}) copy-start(bf16[40,5120]{1,0:T(8,128)(2,1)} %param.16) | copy-start | bytes 1228804
  8.7 213.3 %reduce-scatter.4.cloned.1.call-start = ((), (), s32[]{:S(2)}) async-start(), calls=%async_computation.5 | async-start | bytes 1392640 | tf_op jit(solution)/shard_map/reduce_scatter | solution.py:107
  11.4 149.7 %copy-start = (f32[5,8,4,1280]{3,1,2,0:T(8,128)}, f32[5,8,4,1280]{3,1,2,0:T(8,128)S(1)}, u32[]{:S(2)}) copy-start(f32[5,8,4,1280]{3,1,2,0:T(8,128)S(1)} %copy.42) | copy-start | bytes 2457604
  79.4 82.4 %copy-start.19 = (bf16[512]{0:T(512)(128)(2,1)S(1)}, bf16[512]{0:T(512)(128)(2,1)}, u32[]{:S(2)}) copy-start(bf16[512]{0:T(512)(128)(2,1)} %param.22) | copy-start | bytes 3076
  79.4 82.5 %copy-start.8 = (bf16[2,8192]{1,0:T(2,128)(2,1)S(1)}, bf16[2,8192]{1,0:T(2,128)(2,1)}, u32[]{:S(2)}) copy-start(bf16[2,8192]{1,0:T(2,128)(2,1)} %param.27) | copy-start | bytes 98308
  79.4 82.5 %copy-start.20 = (s32[40]{0:T(128)S(1)}, s32[40]{0:T(128)}, u32[]{:S(2)}) copy-start(s32[40]{0:T(128)} %param.23) | copy-start | bytes 484
  161.1 127.0 %all-gather.9.cloned.1.call-start = ((), (), s32[]{:S(2)}) async-start(), calls=%async_computation.6 | async-start | bytes 4456448 | tf_op jit(solution)/shard_map/all_gather | solution.py:76
  252.0 158.9 %reduce-scatter.6.cloned.1.call-start = ((), (), s32[]{:S(2)}) async-start(), calls=%async_computation.7 | async-start | bytes 8912896 | tf_op jit(solution)/shard_map/reduce_scatter | solution.py:89
  257.8 6.4 copy-start.15
  264.4 39.0 %copy-start.9 = (pred[256,256]{0,1:T(8,128)(4,1)}, pred[256,256]{0,1:T(8,128)(4,1)S(1)}, u32[]{:S(2)}) copy-start(pred[256,256]{0,1:T(8,128)(4,1)S(1)} %fusion.36) | copy-start | bytes 196612
  288.1 10.2 %copy-start.4 = (bf16[256,8192]{1,0:T(8,128)(2,1)S(1)}, bf16[256,8192]{1,0:T(8,128)(2,1)}, u32[]{:S(2)}) copy-start(bf16[256,8192]{1,0:T(8,128)(2,1)} %copy.26) | copy-start | bytes 12582916
  298.2 3.6 copy-start.13
  298.2 3.6 copy-start.14
  301.8 0.6 copy-start.12
  313.0 164.4 %all-gather.11.cloned.1.call-start = ((), (), s32[]{:S(2)}) async-start(), calls=%async_computation.8 | async-start | bytes 4456448 | tf_op jit(solution)/shard_map/all_gather | solution.py:76
  441.6 158.2 %all-reduce.2.cloned.1.call-start = ((), (), s32[]{:S(2)}) async-start(), calls=%async_computation.10 | async-start | bytes 1638400 | tf_op jit(solution)/shard_map/psum | solution.py:119
  441.8 6.5 copy-start.7
  455.9 242.8 %reduce-scatter.8.cloned.1.call-start = ((), (), s32[]{:S(2)}) async-start(), calls=%async_computation.9 | async-start | bytes 8912896 | tf_op jit(solution)/shard_map/reduce_scatter | solution.py:89
  477.5 10.1 %copy-start.3 = (bf16[256,8192]{1,0:T(8,128)(2,1)S(1)}, bf16[256,8192]{1,0:T(8,128)(2,1)}, u32[]{:S(2)}) copy-start(bf16[256,8192]{1,0:T(8,128)(2,1)} %copy.30) | copy-start | bytes 12582916
  487.6 4.2 copy-start.10
  491.2 0.6 copy-start.11
  601.3 1.7 copy-start.1
  601.3 1.7 copy-start.6
  602.6 96.1 %copy-start.2 = (f32[512,256]{0,1:T(8,128)S(1)}, f32[512,256]{0,1:T(8,128)}, u32[]{:S(2)}) copy-start(f32[512,256]{0,1:T(8,128)} %reduce-scatter.6.cloned.1.call-done) | copy-start | bytes 1572868
Sparse Core Ops, SparseCore 0:
  10.4 65.9 all-gather.4
  78.6 77.7 all-gather.6
  161.2 60.7 reduce-scatter.3
  252.1 35.9 all-gather.8
  313.2 97.6 reduce-scatter.5
  441.7 35.7 all-gather.10
  480.5 119.1 all-reduce.1
  602.1 96.5 reduce-scatter.7
where the time goes:
time: 709 us; the launch traced here: 708 us
  waiting for transfers between devices  538 us (76%)
  blocking collectives  66.9 us (9%)
  matrix products  52.9 us (7%)
  local copies, waits for them, and re-layouts  24.3 us (3%)
  between operations  15.3 us (2%)
  other arithmetic  9.97 us (1%)
    reduce_scatter x2, waiting for transfers between devices, section_features(): lax.psum_scatter(lax.dot_general(o_local, attended, (((0,), (1,)), ((), (...  192 us
    psum x1, waiting for transfers between devices, merger_back(): normed_grads = lax.psum(normed_grads, ('sec', 'mp'))  97.3 us
    all_gather x1, waiting for transfers between devices, local(): lax.all_gather(w_out, 'dp', axis=1, tiled=True)  77 us
    all_gather x1, waiting for transfers between devices, local(): lax.all_gather(w_in, 'dp', axis=0, tiled=True)  64.8 us
    reduce_scatter x1, waiting for transfers between devices, merger_front(): lax.psum_scatter(partial_out, ('sec', 'mp'), scatter_dimension=1, tiled=T...  60 us
    psum x2, blocking collectives, section_features(): lax.psum(jnp.sum(rows_local * rows_local, axis=1), ('sec', 'mp'))  55.3 us
    all_gather x2, waiting for transfers between devices, gather_features(): return lax.all_gather(rows_local, ('sec', 'mp'), axis=1, tiled=True)  44.8 us
    dot_general x3, local copies, waits for them, and re-layouts, attend(): jnp.dot(normed, q_local, preferred_element_type=jnp.float32)  18.6 us
  transfers between devices with their start and end apart: 8, of which 8 were waited for; matrix products, arithmetic and copies ran while one was open for 8% of the time, Pallas kernels for 0%

commit v1 on v0

--- a/solution.py
+++ b/solution.py
@@ -78,7 +78,9 @@
 
 def section_features(rows_local, gain_row, allowed, positions, q_local, kv_local, o_local):
     share = rows_local.shape[1]
-    square_sums = lax.psum(jnp.sum(rows_local * rows_local, axis=1), ("sec", "mp"))
+    square_sums = jnp.sum(
+        lax.all_gather(jnp.sum(rows_local * rows_local, axis=1), ("sec", "mp")), axis=0
+    )
     factor = lax.rsqrt(square_sums / D + rms_eps)
     gain_local = lax.dynamic_slice_in_dim(
         gain_row, lax.axis_index(("sec", "mp")) * share, share, 0

time: 709 us -> 686 us (0.968)
  blocking collectives: 66.9 us -> 44.1 us
    psum x2 -> x0, blocking collectives: 55.3 us -> none  [section_features(): lax.psum(jnp.sum(rows_local * rows_local, axis=1), ('sec', 'mp'))]
    all_gather x0 -> x2, blocking collectives: none -> 32.5 us  [section_features(): lax.all_gather(jnp.sum(rows_local * rows_local, axis=1), ('sec', 'mp'))]
where the time goes in v1:
time: 686 us; the launch traced here: 685 us
  waiting for transfers between devices  538 us (78%)
  matrix products  52.9 us (8%)
  blocking collectives  44.1 us (6%)
  local copies, waits for them, and re-layouts  24.3 us (4%)
  between operations  15.3 us (2%)
  other arithmetic  10 us (1%)
    reduce_scatter x2, waiting for transfers between devices, section_features(): lax.psum_scatter(lax.dot_general(o_local, attended, (((0,), (1,)), ((), (...  192 us
    psum x1, waiting for transfers between devices, merger_back(): normed_grads = lax.psum(normed_grads, ('sec', 'mp'))  97.2 us
    all_gather x1, waiting for transfers between devices, local(): lax.all_gather(w_out, 'dp', axis=1, tiled=True)  77 us
    all_gather x1, waiting for transfers between devices, local(): lax.all_gather(w_in, 'dp', axis=0, tiled=True)  64.8 us
    reduce_scatter x1, waiting for transfers between devices, merger_front(): lax.psum_scatter(partial_out, ('sec', 'mp'), scatter_dimension=1, tiled=T...  60 us
    all_gather x2, waiting for transfers between devices, gather_features(): return lax.all_gather(rows_local, ('sec', 'mp'), axis=1, tiled=True)  45.3 us
    all_gather x2, blocking collectives, section_features(): lax.all_gather(jnp.sum(rows_local * rows_local, axis=1), ('sec', 'mp'))  32.5 us
    dot_general x3, local copies, waits for them, and re-layouts, attend(): jnp.dot(normed, q_local, preferred_element_type=jnp.float32)  18.6 us
  transfers between devices with their start and end apart: 8, of which 8 were waited for; matrix products, arithmetic and copies ran while one was open for 8% of the time, Pallas kernels for 0%

profile of v1, /device:TPU:0, one launch (start us, length us, event | category | flops | bytes accessed | tf_op | source)
XLA Modules:
  0.0 685.3 jit_solution(261869376354673570)
XLA Ops:
  7.2 0.7 all-gather.9.cloned.1.call-update
  8.0 0.7 all-gather.11.cloned.1.call-update
  8.7 1.4 reshape.231
  10.2 0.2 reduce_sum.97
  10.4 0.4 multiply_reduce_fusion.1
  10.7 0.2 mul.308
  10.9 0.1 copy.51
  11.1 0.2 sub.50
  11.3 0.1 copy.50
  11.5 64.8 %all-gather.9.cloned.1.call-done = bf16[5120,320]{0,1:T(8,128)(2,1)} async-done(((bf16[640,320]{0,1:T(8,128)(2,1)}), bf16[5120,320]{0,1:T(8,128)(2,1)}) %all-gather.9.cloned.1.call-update) | async-done | bytes 3276816 | tf_op jit(solution)/shard_map/all_gather | solution.py:147
  76.3 3.0 convolution_add_fusion
  79.4 77.0 %all-gather.11.cloned.1.call-done = bf16[320,8192]{1,0:T(8,128)(2,1)} async-done(((bf16[320,1024]{1,0:T(8,128)(2,1)}), bf16[320,8192]{1,0:T(8,128)(2,1)}) %all-gather.11.cloned.1.call-update) | async-done | bytes 5242896 | tf_op jit(solution)/shard_map/all_gather | solution.py:148
  156.4 4.6 fusion.88
  161.1 0.0 all-gather.13.cloned.1.call-start
  161.9 0.1 fusion.116
  161.9 0.1 fusion.87
  162.0 60.0 %reduce-scatter.4.cloned.1.call-done = f32[40,512]{1,0:T(8,128)} async-done(((f32[40,8192]{1,0:T(8,128)}), f32[40,512]{1,0:T(8,128)}) %reduce-scatter.4.cloned.1.call-update) | async-done | bytes 81936 | tf_op jit(solution)/shard_map/reduce_scatter | solution.py:109
  222.0 1.4 multiply_reduce_fusion.3
  223.4 16.0 %all-gather.2 = f32[16,1,256]{2,1,0:T(1,128)S(1)} all-gather(f32[1,1,256]{2,1,0:T(1,128)S(1)} %bitcast.137), channel_id=2, replica_groups=mesh['sec'=4,'dp'=8,'mp'=4] {'sec','mp'}, dimensions={0}, use_global_device_ids=true | all-gather | bytes 17408 | tf_op jit(solution)/shard_map/all_gather | solution.py:82
  239.5 0.8 multiply_convert_fusion.1
  240.4 5.7 slice_bitcast_fusion.1
  246.1 6.4 copy.34
  252.5 0.1 convert_reduce_fusion
  252.7 0.1 fusion.36
  252.8 0.3 multiply_cosine_fusion
  253.1 23.6 %all-gather.13.cloned.1.call-done = bf16[256,8192]{1,0:T(8,128)(2,1)} async-done(((bf16[256,512]{1,0:T(8,128)(2,1)}), bf16[256,8192]{1,0:T(8,128)(2,1)}) %all-gather.13.cloned.1.call-update) | async-done | bytes 4194320 | tf_op jit(solution)/shard_map/all_gather | solution.py:76
  276.7 4.0 fusion.10
  280.7 5.8 all_gather.35
  286.5 0.3 fusion.52
  286.9 3.5 fusion.8
  290.4 0.6 copy-done.12
  291.0 1.1 fusion.21
  292.1 1.2 fusion.117
  293.3 1.6 convolution_convert_fusion.1
  294.9 6.7 convolution_bitcast_fusion.1
  301.7 97.8 %reduce-scatter.6.cloned.1.call-done = f32[512,256]{0,1:T(8,128)} async-done(((f32[8192,256]{0,1:T(8,128)}), f32[512,256]{0,1:T(8,128)}) %reduce-scatter.6.cloned.1.call-update) | async-done | bytes 524304 | tf_op jit(solution)/shard_map/reduce_scatter | solution.py:91
  399.5 1.2 multiply_reduce_fusion.2
  400.7 16.5 %all-gather.3 = f32[16,1,256]{2,1,0:T(1,128)S(1)} all-gather(f32[1,1,256]{2,1,0:T(1,128)S(1)} %bitcast.138), channel_id=3, replica_groups=mesh['sec'=4,'dp'=8,'mp'=4] {'sec','mp'}, dimensions={0}, use_global_device_ids=true | all-gather | bytes 17408 | tf_op jit(solution)/shard_map/all_gather | solution.py:82
  417.3 1.9 multiply_convert_fusion
  419.1 0.2 all-reduce.2.cloned.1.call-start
  419.4 6.5 copy.38
  425.8 7.6 %fusion.71 = f32[40,5120]{1,0:T(8,128)} fusion(bf16[5120,320]{0,1:T(8,128)(2,1)} %all-gather.9.cloned.1.call-done, bf16[320,8192]{1,0:T(8,128)(2,1)} %all-gather.11.cloned.1.call-done, bf16[40,8192]{1,0:T(8,128)(2,1)S(1)} %copy-done.7, pred[40]{0:T(512)(128)(4,1)S(1)} %iota_compare_fusion.2, f32[40,320]{1,0:T(8,128)S(1)} %convolution_add_fusion), kind=kOutput, calls=%fused_computation.107 | convolution fusion | flops 342036480 | bytes 10045480 | tf_op jit(solution)/shard_map/dot_general | solution.py:118
  433.5 0.0 reduce-scatter.8.cloned.1.call-start
  433.5 21.7 %all-gather.15.cloned.1.call-done = bf16[256,8192]{1,0:T(8,128)(2,1)} async-done(((bf16[256,512]{1,0:T(8,128)(2,1)}), bf16[256,8192]{1,0:T(8,128)(2,1)}) %all-gather.15.cloned.1.call-update) | async-done | bytes 4194320 | tf_op jit(solution)/shard_map/all_gather | solution.py:76
  455.3 4.0 fusion.5
  459.3 5.8 all_gather.39
  465.1 0.3 fusion.56
  465.4 3.5 fusion.3
  469.0 0.6 copy-done.11
  469.6 1.0 fusion.19
  470.7 1.2 fusion.120
  471.9 1.6 convolution_convert_fusion
  473.5 6.7 convolution_bitcast_fusion
  480.2 97.2 %all-reduce.2.cloned.1.call-done = f32[40,5120]{1,0:T(8,128)} async-done(((f32[40,5120]{1,0:T(8,128)}), f32[40,5120]{1,0:T(8,128)}) %all-reduce.2.cloned.1.call-update) | async-done | bytes 819216 | tf_op jit(solution)/shard_map/psum | solution.py:121
  577.5 1.5 reshape.234
  579.1 0.4 multiply_reduce_fusion
  579.5 0.6 fusion.29
  580.0 0.2 broadcast_in_dim.45
  580.2 0.1 copy.53
  580.4 0.2 broadcast_in_dim.43
  580.6 0.1 copy.52
  580.7 1.2 fusion.28
  581.9 94.5 %reduce-scatter.8.cloned.1.call-done = f32[512,256]{0,1:T(8,128)} async-done(((f32[8192,256]{0,1:T(8,128)}), f32[512,256]{0,1:T(8,128)}) %reduce-scatter.8.cloned.1.call-update) | async-done | bytes 524304 | tf_op jit(solution)/shard_map/reduce_scatter | solution.py:91
  676.5 2.0 bitcast_add_fusion
  (73 shorter events, 0.7 us)
Async XLA Ops:
  7.2 69.2 %all-gather.9.cloned.1.call-start = ((), (), s32[]{:S(2)}) async-start(), calls=%async_computation.3 | async-start | bytes 3686400 | tf_op jit(solution)/shard_map/all_gather | solution.py:147
  7.9 3.5 copy-start.16
  7.9 3.6 copy-start.17
  7.9 148.5 %all-gather.11.cloned.1.call-start = ((), (), s32[]{:S(2)}) async-start(), calls=%async_computation.4 | async-start | bytes 5898240 | tf_op jit(solution)/shard_map/all_gather | solution.py:148
  8.7 2.8 copy-start.18
  8.7 67.7 %copy-start.5 = (bf16[40,5120]{1,0:T(8,128)(2,1)S(1)}, bf16[40,5120]{1,0:T(8,128)(2,1)}, u32[]{:S(2)}) copy-start(bf16[40,5120]{1,0:T(8,128)(2,1)} %param.16) | copy-start | bytes 1228804
  8.7 213.3 %reduce-scatter.4.cloned.1.call-start = ((), (), s32[]{:S(2)}) async-start(), calls=%async_computation.5 | async-start | bytes 1392640 | tf_op jit(solution)/shard_map/reduce_scatter | solution.py:109
  11.4 149.7 %copy-start = (f32[5,8,4,1280]{3,1,2,0:T(8,128)}, f32[5,8,4,1280]{3,1,2,0:T(8,128)S(1)}, u32[]{:S(2)}) copy-start(f32[5,8,4,1280]{3,1,2,0:T(8,128)S(1)} %copy.50) | copy-start | bytes 2457604
  79.4 82.4 %copy-start.19 = (bf16[512]{0:T(512)(128)(2,1)S(1)}, bf16[512]{0:T(512)(128)(2,1)}, u32[]{:S(2)}) copy-start(bf16[512]{0:T(512)(128)(2,1)} %param.22) | copy-start | bytes 3076
  79.4 82.5 %copy-start.8 = (bf16[2,8192]{1,0:T(2,128)(2,1)S(1)}, bf16[2,8192]{1,0:T(2,128)(2,1)}, u32[]{:S(2)}) copy-start(bf16[2,8192]{1,0:T(2,128)(2,1)} %param.27) | copy-start | bytes 98308
  79.4 82.5 %copy-start.20 = (s32[40]{0:T(128)S(1)}, s32[40]{0:T(128)}, u32[]{:S(2)}) copy-start(s32[40]{0:T(128)} %param.23) | copy-start | bytes 484
  161.1 115.6 %all-gather.13.cloned.1.call-start = ((), (), s32[]{:S(2)}) async-start(), calls=%async_computation.6 | async-start | bytes 4456448 | tf_op jit(solution)/shard_map/all_gather | solution.py:76
  240.3 159.2 %reduce-scatter.6.cloned.1.call-start = ((), (), s32[]{:S(2)}) async-start(), calls=%async_computation.7 | async-start | bytes 8912896 | tf_op jit(solution)/shard_map/reduce_scatter | solution.py:91
  246.1 6.4 copy-start.15
  252.8 39.3 %copy-start.9 = (pred[256,256]{0,1:T(8,128)(4,1)}, pred[256,256]{0,1:T(8,128)(4,1)S(1)}, u32[]{:S(2)}) copy-start(pred[256,256]{0,1:T(8,128)(4,1)S(1)} %fusion.36) | copy-start | bytes 196612
  276.7 10.2 %copy-start.4 = (bf16[256,8192]{1,0:T(8,128)(2,1)S(1)}, bf16[256,8192]{1,0:T(8,128)(2,1)}, u32[]{:S(2)}) copy-start(bf16[256,8192]{1,0:T(8,128)(2,1)} %copy.34) | copy-start | bytes 12582916
  286.8 3.6 copy-start.13
  286.8 3.6 copy-start.14
  290.4 0.6 copy-start.12
  301.7 153.6 %all-gather.15.cloned.1.call-start = ((), (), s32[]{:S(2)}) async-start(), calls=%async_computation.8 | async-start | bytes 4456448 | tf_op jit(solution)/shard_map/all_gather | solution.py:76
  419.1 158.3 %all-reduce.2.cloned.1.call-start = ((), (), s32[]{:S(2)}) async-start(), calls=%async_computation.10 | async-start | bytes 1638400 | tf_op jit(solution)/shard_map/psum | solution.py:121
  419.4 6.5 copy-start.7
  433.5 243.0 %reduce-scatter.8.cloned.1.call-start = ((), (), s32[]{:S(2)}) async-start(), calls=%async_computation.9 | async-start | bytes 8912896 | tf_op jit(solution)/shard_map/reduce_scatter | solution.py:91
  455.3 10.1 %copy-start.3 = (bf16[256,8192]{1,0:T(8,128)(2,1)S(1)}, bf16[256,8192]{1,0:T(8,128)(2,1)}, u32[]{:S(2)}) copy-start(bf16[256,8192]{1,0:T(8,128)(2,1)} %copy.38) | copy-start | bytes 12582916
  465.4 4.2 copy-start.10
  469.0 0.6 copy-start.11
  579.0 1.7 copy-start.1
  579.0 1.7 copy-start.6
  580.4 96.1 %copy-start.2 = (f32[512,256]{0,1:T(8,128)S(1)}, f32[512,256]{0,1:T(8,128)}, u32[]{:S(2)}) copy-start(f32[512,256]{0,1:T(8,128)} %reduce-scatter.6.cloned.1.call-done) | copy-start | bytes 1572868
Sparse Core Ops, SparseCore 0:
  10.4 65.9 all-gather.8
  78.6 77.7 all-gather.10
  161.2 60.7 reduce-scatter.3
  240.4 36.2 all-gather.12
  301.8 97.6 reduce-scatter.5
  419.3 35.9 all-gather.14
  458.3 119.0 all-reduce.1
  579.9 96.5 reduce-scatter.7
